TPU v7x, 32 devices: a whole 2x2x4 slice. The times are simulated.
32 devices in a mesh: grp: 4 (over y, x), freq: 8 (over z, core).
Axes of the slice: x: 2, y: 2, z: 4, core: 2. Of those that a mesh axis runs over, the one named last changes fastest.
Arguments:
- transfer: bfloat16 [512, 2, 128, 512], P('freq', None, 'grp'), may hold values from -0.1875 to 0.1875
- adjoint: bfloat16 [512, 2, 512, 128], P('freq'), may hold values from -6 to 6
- lower_rows: bfloat16 [131072, 384], P(('grp', 'freq')), may hold values from -6 to 6
- pivot_store: bfloat16 [512, 384], P('grp'), may hold values from -0.3125 to 0.3125
- owners: int32 [3], replicated, may hold values from 0 to 3
- inverse_factor: bfloat16 [128, 128], replicated, as said below
Outputs:
- panel: bfloat16 [131072, 128], P(('grp', 'freq'))
Inputs may be any that keep to these rules, and one draw needn't show every extreme that they name: `inverse_factor`: upper triangular, with diagonal entries from 0.5 to 2.
All inputs are finite; a program needn't handle non-finite values.
Results may differ from a plain program's by a relative error of at most 0.0059.
Values may be sent and summed in bfloat16 or wider, within the bound.
A program may use at most 64 MiB of HBM per device.

v0:
```python
import functools
import math

import jax
import jax.numpy as jnp
from jax import lax
from jax.experimental import pallas as pl
from jax.experimental.pallas import tpu as pltpu
from jax.sharding import PartitionSpec as P

MESH = pl.DeviceIdType.MESH
CHUNK = 8
AHEAD = 3
TILE = 1024
VMEM_BYTES = 64 * 1024 * 1024
SPARE = 11 * 1024 * 1024
COARSE = 32


def flip(me, mask):
    bit = 1
    other = me
    while bit <= mask:
        if mask & bit:
            other = other + bit * (1 - 2 * lax.rem(me // bit, 2))
        bit *= 2
    return other


def kernel(
    nf, ng, kc,
    owners_hbm, tr_hbm, ad_hbm, lo_hbm, pv_hbm, out_ref,
    owners, tr, ad, lo, pv, spec, sbuf, rbuf, table, acc,
    in_sem, owners_sem, lo_sem, pv_sem, own_sem, send_sem, recv_sem, psend_sem, precv_sem,
):
    kl, _, sl, _ = tr.shape
    c = ad.shape[3]
    nch = kl // kc
    s_loc = sl // nf
    nt, width = acc.shape
    me = lax.axis_index("freq")
    grp = lax.axis_index("grp")

    def loads(j):
        rows = pl.ds(j * kc, kc)
        return (
            pltpu.make_async_copy(tr_hbm.at[rows], tr.at[rows], in_sem.at[j, 0]),
            pltpu.make_async_copy(ad_hbm.at[rows], ad.at[rows], in_sem.at[j, 1]),
        )

    lo_copy = pltpu.make_async_copy(lo_hbm, lo, lo_sem)
    owners_copy = pltpu.make_async_copy(owners_hbm, owners, owners_sem)
    pv_copy = pltpu.make_async_copy(pv_hbm, pv.at[grp], pv_sem)

    for copy in loads(0):
        copy.start()

    barrier = pltpu.get_barrier_semaphore()
    for mask in range(1, nf):
        pl.semaphore_signal(barrier, inc=1, device_id={"freq": flip(me, mask)}, device_id_type=MESH)
    for mask in range(1, ng):
        pl.semaphore_signal(barrier, inc=1, device_id={"grp": flip(grp, mask)}, device_id_type=MESH)

    def spectra(j):
        for i in range(kc):
            k = j * kc + i
            right = jnp.concatenate([ad[k, 0], ad[k, 1]], axis=1)
            left = jnp.concatenate([tr[k, 0], tr[k, 1]], axis=0)
            both = jnp.dot(left, right, preferred_element_type=jnp.float32)
            spec[0, pl.ds(i * sl, sl), :] = both[:sl, :c] - both[sl:, c:]
            spec[1, pl.ds(i * sl, sl), :] = both[:sl, c:] + both[sl:, :c]
        for d in range(nf):
            for s in range(s_loc):
                rows = pl.ds(d * s_loc + s, kc, stride=sl)
                block = jnp.concatenate([spec[0, rows, :], spec[1, rows, :]], axis=0)
                sbuf[j, d, :, s * c:(s + 1) * c] = block.astype(jnp.bfloat16)

    def own_copy(j):
        return pltpu.make_async_copy(sbuf.at[j, me], rbuf.at[j, me], own_sem.at[j])

    def remote(j, mask):
        return pltpu.make_async_remote_copy(
            src_ref=sbuf.at[j, flip(me, mask)],
            dst_ref=rbuf.at[j, me],
            send_sem=send_sem.at[j, mask],
            recv_sem=recv_sem.at[j, mask],
            device_id={"freq": flip(me, mask)},
            device_id_type=MESH,
        )

    def arrival(j, mask):
        other = flip(me, mask)
        return pltpu.make_async_remote_copy(
            src_ref=sbuf.at[j, other],
            dst_ref=rbuf.at[j, other],
            send_sem=send_sem.at[j, mask],
            recv_sem=recv_sem.at[j, mask],
            device_id={"freq": other},
            device_id_type=MESH,
        )

    def pivot_copy(mask, slot):
        return pltpu.make_async_remote_copy(
            src_ref=pv_hbm,
            dst_ref=pv.at[slot],
            send_sem=psend_sem.at[mask],
            recv_sem=precv_sem.at[mask],
            device_id={"grp": flip(grp, mask)},
            device_id_type=MESH,
        )

    far = tuple(range(nf - 1, nf // 2 - 1, -1))
    near = tuple(range(nf // 2 - 1, 0, -1))
    def send(j, masks):
        for mask in masks:
            remote(j, mask).start()
        own_copy(j).start()

    for copy in loads(0):
        copy.wait()
    for j in range(1, min(AHEAD, nch)):
        for copy in loads(j):
            copy.start()
    spectra(0)
    pl.semaphore_wait(barrier, nf - 1 + ng - 1)
    send(0, far + near)

    @pl.loop(1, nch)
    def _(j):
        @pl.when(j + AHEAD - 1 < nch)
        def _():
            for copy in loads(j + AHEAD - 1):
                copy.start()

        for copy in loads(j):
            copy.wait()
        spectra(j)
        send(j, near + far)

    owners_copy.start()
    pv_copy.start()
    lo_copy.start()
    for mask in range(1, ng):
        pivot_copy(mask, grp).start()

    cols = nf * 2 * kc
    coarse = nt // COARSE
    scale = 1.0 / math.sqrt(kl * nf)
    turn = 2.0 * math.pi / nt

    @pl.loop(0, nch)
    def _(j):
        def phase(rows, step, shift):
            col = lax.broadcasted_iota(jnp.int32, (rows, cols), 1)
            row = lax.broadcasted_iota(jnp.int32, (rows, cols), 0) * step
            kk = (col // (2 * kc)) * kl + j * kc + col % kc
            q = (col // kc) % 2
            whole = kk * row + q * shift
            return (whole % nt).astype(jnp.float32) * turn

        high = phase(coarse, COARSE, 0)
        low = phase(COARSE, 1, nt // 4)
        cos_high, sin_high = jnp.cos(high) * scale, jnp.sin(high) * scale
        cos_low, sin_low = jnp.cos(low), jnp.sin(low)
        for a in range(coarse):
            value = cos_high[a:a + 1] * cos_low - sin_high[a:a + 1] * sin_low
            table[j, a * COARSE:(a + 1) * COARSE, :] = value.astype(jnp.bfloat16)

    lo_copy.wait()
    owners_copy.wait()
    pv_copy.wait()
    for mask in range(1, ng):
        pivot_copy(mask, flip(grp, mask)).wait_recv()
    panels = lo.shape[1] // c
    pivots = jnp.concatenate(
        [pv[owners[p], :, p * c:(p + 1) * c] for p in range(panels)], axis=1
    )
    tile = min(TILE, nt)

    for s in range(s_loc):
        @pl.loop(0, nt // tile)
        def _(i):
            rows = lo[pl.ds(pl.multiple_of(s * nt + i * tile, tile), tile), :]
            update = lax.dot_general(
                rows, pivots, (((1,), (1,)), ((), ())), preferred_element_type=jnp.float32
            )
            acc[pl.ds(pl.multiple_of(i * tile, tile), tile), s * c:(s + 1) * c] = -update

    def arrive(j):
        for mask in range(nf - 1, 0, -1):
            arrival(j, mask).wait_recv()
        own_copy(j).wait()

    def term(j, i):
        rows = pl.ds(pl.multiple_of(i * tile, tile), tile)
        right = rbuf[j].reshape(cols, width)
        return acc[rows, :] + jnp.dot(table[j, rows, :], right, preferred_element_type=jnp.float32)

    @pl.loop(0, nch - 1)
    def _(j):
        arrive(j)

        @pl.loop(0, nt // tile)
        def _(i):
            acc[pl.ds(pl.multiple_of(i * tile, tile), tile), :] = term(j, i)

    last = nch - 1
    arrive(last)

    @pl.loop(0, nt // tile)
    def _(i):
        value = term(last, i).astype(jnp.bfloat16)
        for s in range(s_loc):
            out_ref[pl.ds(pl.multiple_of(s * nt + i * tile, tile), tile), :] = value[:, s * c:(s + 1) * c]

    @pl.loop(0, nch)
    def _(j):
        for mask in range(nf - 1, 0, -1):
            remote(j, mask).wait_send()

    for mask in range(1, ng):
        pivot_copy(mask, grp).wait_send()


def per_device(nf, ng, transfer, adjoint, lower_rows, pivot_store, owners, inverse_factor):
    kl, _, sl, m = transfer.shape
    c = adjoint.shape[3]
    kc = min(CHUNK, kl)
    nch = kl // kc
    s_loc = sl // nf
    rows = lower_rows.shape[0]
    nt = rows // s_loc
    bf16 = jnp.bfloat16
    in_hbm = lambda x: pltpu.with_memory_space_constraint(x, pltpu.HBM)
    reduced = pl.pallas_call(
        functools.partial(kernel, nf, ng, kc),
        out_shape=jax.ShapeDtypeStruct((rows, c), bf16),
        in_specs=[pl.BlockSpec(memory_space=pltpu.HBM)] * 5,
        out_specs=pl.BlockSpec(memory_space=pltpu.VMEM),
        scratch_shapes=[
            pltpu.SMEM(owners.shape, jnp.int32),
            pltpu.VMEM(transfer.shape, bf16),
            pltpu.VMEM(adjoint.shape, bf16),
            pltpu.VMEM(lower_rows.shape, bf16),
            pltpu.VMEM((ng,) + pivot_store.shape, bf16),
            pltpu.VMEM((2, kc * sl, c), jnp.float32),
            pltpu.VMEM((nch, nf, 2 * kc, s_loc * c), bf16),
            pltpu.VMEM((nch, nf, 2 * kc, s_loc * c), bf16),
            pltpu.VMEM((nch, nt, nf * 2 * kc), bf16),
            pltpu.VMEM((nt, s_loc * c), jnp.float32),
            pltpu.SemaphoreType.DMA((nch, 2)),
            pltpu.SemaphoreType.DMA,
            pltpu.SemaphoreType.DMA,
            pltpu.SemaphoreType.DMA,
            pltpu.SemaphoreType.DMA((nch,)),
            pltpu.SemaphoreType.DMA((nch, nf)),
            pltpu.SemaphoreType.DMA((nch, nf)),
            pltpu.SemaphoreType.DMA((ng,)),
            pltpu.SemaphoreType.DMA((ng,)),
        ],
        compiler_params=pltpu.CompilerParams(
            collective_id=0, has_side_effects=True, vmem_limit_bytes=VMEM_BYTES - 2 * rows * c - SPARE
        ),
    )(in_hbm(owners), transfer, adjoint, lower_rows, in_hbm(pivot_store))
    return jnp.dot(reduced, inverse_factor, preferred_element_type=jnp.float32).astype(bf16)


def solution(mesh):
    nf, ng = mesh.shape["freq"], mesh.shape["grp"]
    in_specs = (
        P("freq", None, "grp", None),
        P("freq", None, None, None),
        P(("grp", "freq"), None),
        P("grp", None),
        P(),
        P(),
    )
    out_specs = P(("grp", "freq"), None)
    return jax.shard_map(
        functools.partial(per_device, nf, ng),
        mesh=mesh, in_specs=in_specs, out_specs=out_specs, check_vma=False,
    )
```

profile of v0, /device:TPU:0, one launch (start us, length us, event | category | flops | bytes accessed | tf_op | source)
XLA Modules:
  0.0 33.3 jit_solution(2269274423763961719)
XLA Ops:
  0.0 0.0 copy-start
  0.0 31.9 %shard_map.64 = bf16[4096,128]{1,0:T(8,128)(2,1)S(1)} custom-call(s32[3]{0:T(128)} %owners_hbm.1, bf16[64,2,32,512]{3,2,1,0:T(8,128)(2,1)} %tr_hbm.1, bf16[64,2,512,128]{3,2,1,0:T(8,128)(2,1)} %ad_hbm.1, bf16[4096,384]{1,0:T(8,128)(2,1)} %lo_hbm.1, bf16[128,384]{1,0:T(8,128)(2,1)} %pv_hbm.1), custom_call_target="tpu_custom_call" | custom-call | tf_op jit(solution)/shard_map/pallas_call | solution.py:235
  31.9 0.0 copy-done
  31.9 1.4 %convolution_convert_fusion = bf16[4096,128]{1,0:T(8,128)(2,1)} fusion(bf16[4096,128]{1,0:T(8,128)(2,1)S(1)} %shard_map.64, bf16[128,128]{1,0:T(8,128)(2,1)S(1)} %copy-done), kind=kOutput, calls=%fused_computation | convolution fusion | flops 134742016 | bytes 2129920 | tf_op jit(solution)/shard_map/dot_general | solution.py:265
Async XLA Ops:
  0.0 31.9 %copy-start = (bf16[128,128]{1,0:T(8,128)(2,1)S(1)}, bf16[128,128]{1,0:T(8,128)(2,1)}, u32[]{:S(2)}) copy-start(bf16[128,128]{1,0:T(8,128)(2,1)} %param.11) | copy-start | bytes 98308
where the time goes:
time: 33.5 us; the launch traced here: 33.3 us
  Pallas kernels  31.9 us (95%)
  matrix products  1.39 us (4%)
    pallas_call x1, Pallas kernels, per_device(): pl.pallas_call(functools.partial(kernel, nf, ng, kc), out_shape=jax.Shape...  31.9 us
    dot_general x1, matrix products, per_device(): jnp.dot(reduced, inverse_factor, preferred_element_type=jnp.float32)  1.39 us

commit v1 on v0

v1 whole, which is shorter than its diff:
```python
import functools
import math

import jax
import jax.numpy as jnp
from jax import lax
from jax.experimental import pallas as pl
from jax.experimental.pallas import tpu as pltpu
from jax.sharding import PartitionSpec as P

MESH = pl.DeviceIdType.MESH
CHUNK = 8
AHEAD = 3
TILE = 256
VMEM_BYTES = 64 * 1024 * 1024
SPARE = 11 * 1024 * 1024
COARSE = 32
QUARTERS = 4


def flip(index, bit):
    return index + bit * (1 - 2 * lax.rem(index // bit, 2))


def kernel(
    nf, ng, kc,
    owners_hbm, tr_hbm, ad_hbm, lo_hbm, pv_hbm, inv_hbm, out_ref,
    owners, tr, ad, lo, pv, inv, spec, sbuf, rbuf, table, acc,
    in_sem, owners_sem, lo_sem, pv_sem, inv_sem, own_sem,
    first_send, first_recv, send_sem, recv_sem, psend_sem, precv_sem,
):
    f32, bf16 = jnp.float32, jnp.bfloat16
    kl, _, sl, _ = tr.shape
    c = ad.shape[3]
    nch = kl // kc
    s_loc = sl // nf
    nt, width = acc.shape
    size = nf // QUARTERS
    me = lax.axis_index("freq")
    grp = lax.axis_index("grp")
    quarter = me // size
    place = lax.rem(me, size)
    end = 1 - lax.rem(quarter // 2 + lax.rem(quarter, 2), 2)
    near = flip(quarter, 1)
    across = flip(quarter, 2)
    other = flip(across, 1)
    far_end = across + end * (other - across)
    far_mid = other + end * (across - other)

    def loads(j):
        rows = pl.ds(j * kc, kc)
        return (
            pltpu.make_async_copy(tr_hbm.at[rows], tr.at[rows], in_sem.at[j, 0]),
            pltpu.make_async_copy(ad_hbm.at[rows], ad.at[rows], in_sem.at[j, 1]),
        )

    lo_copy = pltpu.make_async_copy(lo_hbm, lo, lo_sem)
    owners_copy = pltpu.make_async_copy(owners_hbm, owners, owners_sem)
    pv_copy = pltpu.make_async_copy(pv_hbm, pv.at[grp], pv_sem)
    inv_copy = pltpu.make_async_copy(inv_hbm, inv, inv_sem)

    inv_copy.start()
    for copy in loads(0):
        copy.start()

    barrier = pltpu.get_barrier_semaphore()
    for step in range(1, nf):
        pl.semaphore_signal(
            barrier, inc=1, device_id={"freq": lax.rem(me + step, nf)}, device_id_type=MESH
        )
    for step in range(1, ng):
        pl.semaphore_signal(
            barrier, inc=1, device_id={"grp": lax.rem(grp + step, ng)}, device_id_type=MESH
        )

    def spectra(j):
        for i in range(kc):
            k = j * kc + i
            right = jnp.concatenate([ad[k, 0], ad[k, 1]], axis=1)
            left = jnp.concatenate([tr[k, 0], tr[k, 1]], axis=0)
            both = jnp.dot(left, right, preferred_element_type=f32)
            spec[0, pl.ds(i * sl, sl), :] = both[:sl, :c] - both[sl:, c:]
            spec[1, pl.ds(i * sl, sl), :] = both[:sl, c:] + both[sl:, :c]
        rows = pl.ds(pl.multiple_of(j * 2 * kc, 2 * kc), 2 * kc)
        factor = inv[...]
        for d in range(nf):
            blocks = []
            for s in range(s_loc):
                picked = pl.ds(d * s_loc + s, kc, stride=sl)
                blocks += [spec[0, picked, :], spec[1, picked, :]]
            block = jnp.concatenate(blocks, axis=0).astype(bf16)
            scaled = jnp.dot(block, factor, preferred_element_type=f32).astype(bf16)
            for s in range(s_loc):
                sbuf[d, rows, s * c:(s + 1) * c] = scaled[s * 2 * kc:(s + 1) * 2 * kc, :]

    def device(q, i):
        return q * size + lax.rem(place + i, size)

    def first(j, i):
        dest = device(far_end, i)
        rows = pl.ds(pl.multiple_of(j * 2 * kc, 2 * kc), 2 * kc)
        return pltpu.make_async_remote_copy(
            src_ref=sbuf.at[dest, rows],
            dst_ref=rbuf.at[me, rows],
            send_sem=first_send.at[j, i],
            recv_sem=first_recv.at[end, j, place],
            device_id={"freq": dest},
            device_id_type=MESH,
        )

    def first_arrival(q, kind, j, i):
        src = q * size + i
        rows = pl.ds(pl.multiple_of(j * 2 * kc, 2 * kc), 2 * kc)
        return pltpu.make_async_remote_copy(
            src_ref=sbuf.at[src, rows],
            dst_ref=rbuf.at[src, rows],
            send_sem=first_send.at[j, i],
            recv_sem=first_recv.at[kind, j, i],
            device_id={"freq": src},
            device_id_type=MESH,
        )

    def whole(q, i):
        dest = device(q, i)
        return pltpu.make_async_remote_copy(
            src_ref=sbuf.at[dest],
            dst_ref=rbuf.at[me],
            send_sem=send_sem.at[dest],
            recv_sem=recv_sem.at[me],
            device_id={"freq": dest},
            device_id_type=MESH,
        )

    def whole_arrival(src):
        return pltpu.make_async_remote_copy(
            src_ref=sbuf.at[src],
            dst_ref=rbuf.at[src],
            send_sem=send_sem.at[src],
            recv_sem=recv_sem.at[src],
            device_id={"freq": src},
            device_id_type=MESH,
        )

    own_copy = pltpu.make_async_copy(sbuf.at[me], rbuf.at[me], own_sem)

    def pivot_copy(step, slot):
        return pltpu.make_async_remote_copy(
            src_ref=pv_hbm,
            dst_ref=pv.at[slot],
            send_sem=psend_sem.at[step],
            recv_sem=precv_sem.at[step],
            device_id={"grp": lax.rem(grp + step, ng)},
            device_id_type=MESH,
        )

    inv_copy.wait()
    for copy in loads(0):
        copy.wait()
    for j in range(1, min(AHEAD, nch)):
        for copy in loads(j):
            copy.start()
    spectra(0)
    pl.semaphore_wait(barrier, nf - 1 + ng - 1)
    for i in range(size):
        first(0, i).start()

    @pl.loop(1, nch)
    def _(j):
        @pl.when(j + AHEAD - 1 < nch)
        def _():
            for copy in loads(j + AHEAD - 1):
                copy.start()

        for copy in loads(j):
            copy.wait()
        spectra(j)
        for i in range(size):
            first(j, i).start()

    for i in range(size):
        whole(far_mid, i).start()
    for i in range(size):
        whole(near, i).start()
    for i in range(1, size):
        whole(quarter, i).start()
    own_copy.start()

    owners_copy.start()
    pv_copy.start()
    lo_copy.start()
    for step in range(1, ng):
        pivot_copy(step, grp).start()

    cols = size * 2 * kl
    coarse = nt // COARSE
    scale = 1.0 / math.sqrt(kl * nf)
    turn = 2.0 * math.pi / nt

    @pl.loop(0, QUARTERS)
    def _(q):
        def phase(rows, step, shift):
            col = lax.broadcasted_iota(jnp.int32, (rows, cols), 1)
            row = lax.broadcasted_iota(jnp.int32, (rows, cols), 0) * step
            kk = q * size * kl + (col // (2 * kc)) * kc + col % kc
            part = (col // kc) % 2
            turns = kk * row + part * shift
            return (turns % nt).astype(f32) * turn

        high = phase(coarse, COARSE, 0)
        low = phase(COARSE, 1, nt // 4)
        cos_high, sin_high = jnp.cos(high) * scale, jnp.sin(high) * scale
        cos_low, sin_low = jnp.cos(low), jnp.sin(low)
        for a in range(coarse):
            value = cos_high[a:a + 1] * cos_low - sin_high[a:a + 1] * sin_low
            table[q, a * COARSE:(a + 1) * COARSE, :] = value.astype(bf16)

    lo_copy.wait()
    owners_copy.wait()
    pv_copy.wait()
    for step in range(1, ng):
        pivot_copy(step, lax.rem(grp + ng - step, ng)).wait_recv()
    panels = lo.shape[1] // c
    pivots = jnp.concatenate(
        [pv[owners[p], :, p * c:(p + 1) * c] for p in range(panels)], axis=1
    )
    turned = jnp.transpose(inv[...].astype(f32)).astype(bf16)
    scaled_pivots = jnp.dot(turned, pivots, preferred_element_type=f32).astype(bf16)
    tile = min(TILE, nt)

    for s in range(s_loc):
        @pl.loop(0, nt // tile)
        def _(i):
            rows = lo[pl.ds(pl.multiple_of(s * nt + i * tile, tile), tile), :]
            update = lax.dot_general(
                rows, scaled_pivots, (((1,), (1,)), ((), ())), preferred_element_type=f32
            )
            acc[pl.ds(pl.multiple_of(i * tile, tile), tile), s * c:(s + 1) * c] = -update

    def term(q, i):
        rows = pl.ds(pl.multiple_of(i * tile, tile), tile)
        right = rbuf[pl.ds(q * size, size)].reshape(cols, width)
        return acc[rows, :] + jnp.dot(table[q, rows, :], right, preferred_element_type=f32)

    def add(q):
        @pl.loop(0, nt // tile)
        def _(i):
            acc[pl.ds(pl.multiple_of(i * tile, tile), tile), :] = term(q, i)

    def wait_whole(q):
        for i in range(size):
            whole_arrival(q * size + i).wait_recv()

    def wait_first(q, kind):
        @pl.loop(0, nch)
        def _(j):
            for i in range(size):
                first_arrival(q, kind, j, i).wait_recv()

    own_copy.wait()
    for i in range(1, size):
        whole_arrival(device(quarter, i)).wait_recv()
    add(quarter)

    wait_whole(near)
    add(near)

    @pl.when(end == 1)
    def _():
        wait_first(far_end, 1)

    @pl.when(end == 0)
    def _():
        wait_whole(far_end)
    add(far_end)

    @pl.when(end == 1)
    def _():
        wait_first(far_mid, 0)

    @pl.when(end == 0)
    def _():
        wait_whole(far_mid)

    @pl.loop(0, nt // tile)
    def _(i):
        value = term(far_mid, i).astype(bf16)
        for s in range(s_loc):
            out_ref[pl.ds(pl.multiple_of(s * nt + i * tile, tile), tile), :] = value[:, s * c:(s + 1) * c]

    @pl.loop(0, nch)
    def _(j):
        for i in range(size):
            first(j, i).wait_send()
    for i in range(size):
        whole(far_mid, i).wait_send()
        whole(near, i).wait_send()
    for i in range(1, size):
        whole(quarter, i).wait_send()
    for step in range(1, ng):
        pivot_copy(step, grp).wait_send()


def per_device(nf, ng, transfer, adjoint, lower_rows, pivot_store, owners, inverse_factor):
    kl, _, sl, m = transfer.shape
    c = adjoint.shape[3]
    kc = min(CHUNK, kl)
    nch = kl // kc
    s_loc = sl // nf
    size = nf // QUARTERS
    rows = lower_rows.shape[0]
    nt = rows // s_loc
    bf16 = jnp.bfloat16
    in_hbm = lambda x: pltpu.with_memory_space_constraint(x, pltpu.HBM)
    dma = pltpu.SemaphoreType.DMA
    return pl.pallas_call(
        functools.partial(kernel, nf, ng, kc),
        out_shape=jax.ShapeDtypeStruct((rows, c), bf16),
        in_specs=[pl.BlockSpec(memory_space=pltpu.HBM)] * 6,
        out_specs=pl.BlockSpec(memory_space=pltpu.VMEM),
        scratch_shapes=[
            pltpu.SMEM(owners.shape, jnp.int32),
            pltpu.VMEM(transfer.shape, bf16),
            pltpu.VMEM(adjoint.shape, bf16),
            pltpu.VMEM(lower_rows.shape, bf16),
            pltpu.VMEM((ng,) + pivot_store.shape, bf16),
            pltpu.VMEM(inverse_factor.shape, bf16),
            pltpu.VMEM((2, kc * sl, c), jnp.float32),
            pltpu.VMEM((nf, 2 * kl, s_loc * c), bf16),
            pltpu.VMEM((nf, 2 * kl, s_loc * c), bf16),
            pltpu.VMEM((QUARTERS, nt, size * 2 * kl), bf16),
            pltpu.VMEM((nt, s_loc * c), jnp.float32),
            dma((nch, 2)), dma, dma, dma, dma, dma,
            dma((nch, size)), dma((2, nch, size)), dma((nf,)), dma((nf,)), dma((ng,)), dma((ng,)),
        ],
        compiler_params=pltpu.CompilerParams(
            collective_id=0, has_side_effects=True, vmem_limit_bytes=VMEM_BYTES - 2 * rows * c - SPARE
        ),
    )(in_hbm(owners), transfer, adjoint, lower_rows, in_hbm(pivot_store), in_hbm(inverse_factor))


def solution(mesh):
    nf, ng = mesh.shape["freq"], mesh.shape["grp"]
    in_specs = (
        P("freq", None, "grp", None),
        P("freq", None, None, None),
        P(("grp", "freq"), None),
        P("grp", None),
        P(),
        P(),
    )
    out_specs = P(("grp", "freq"), None)
    return jax.shard_map(
        functools.partial(per_device, nf, ng),
        mesh=mesh, in_specs=in_specs, out_specs=out_specs, check_vma=False,
    )
```

time: 33.5 us -> 31.1 us (0.928)
  the two profiles are of different devices: /device:TPU:0 before, /device:TPU:9 now
where the time goes in v1:
time: 31.1 us; the launch traced here: 30.9 us
  Pallas kernels  29.9 us (96%)
  local copies, waits for them, and re-layouts  0.97 us (3%)
    pallas_call x1, Pallas kernels, per_device(): pl.pallas_call(functools.partial(kernel, nf, ng, kc), out_shape=jax.Shape...  29.9 us
    unnamed x1, local copies, waits for them, and re-layouts  0.97 us

profile of v1, /device:TPU:9, one launch (start us, length us, event | category | flops | bytes accessed | tf_op | source)
XLA Modules:
  0.0 30.9 jit_solution(18360432699090492619)
XLA Ops:
  0.0 29.9 %shard_map.64 = bf16[4096,128]{1,0:T(8,128)(2,1)S(1)} custom-call(s32[3]{0:T(128)} %owners_hbm.1, bf16[64,2,32,512]{3,2,1,0:T(8,128)(2,1)} %tr_hbm.1, bf16[64,2,512,128]{3,2,1,0:T(8,128)(2,1)} %ad_hbm.1, bf16[4096,384]{1,0:T(8,128)(2,1)} %lo_hbm.1, bf16[128,384]{1,0:T(8,128)(2,1)} %pv_hbm.1, bf16[128,128]{1,0:T(8,128)(2,1)} %inv_hbm.1), custom_call_target="tpu_custom_call" | custom-call | tf_op jit(solution)/shard_map/pallas_call | solution.py:315
  29.9 1.0 %copy.8 = bf16[4096,128]{1,0:T(8,128)(2,1)} copy(bf16[4096,128]{1,0:T(8,128)(2,1)S(1)} %shard_map.64) | data formatting | bytes 2097152

commit v2 on v1

v2 whole, which is shorter than its diff:
```python
import functools
import math

import jax
import jax.numpy as jnp
from jax import lax
from jax.experimental import pallas as pl
from jax.experimental.pallas import tpu as pltpu
from jax.sharding import PartitionSpec as P

MESH = pl.DeviceIdType.MESH
CHUNK = 8
AHEAD = 4
PARTS = 4
HALVES = 2
LEAD = 2
NEAR_MESSAGES = 4
TILE = 1024
VMEM_BYTES = 64 * 1024 * 1024
SPARE = 11 * 1024 * 1024
LAST_BYTES = 4 * 1024 * 1024
COARSE = 32
QUARTERS = 4


def flip(index, bit):
    return index + bit * (1 - 2 * lax.rem(index // bit, 2))


def half_block(ref, q, h, size):
    block = ref[pl.ds(q * size, size), h]
    return block.reshape(block.shape[0] * block.shape[1], block.shape[2])


def finished(acc, table, rbuf, q, h, size):
    part = acc.shape[1] // HALVES
    right = half_block(rbuf, q, h, size)
    return acc[:, h * part:(h + 1) * part] + jnp.dot(table[...], right, preferred_element_type=jnp.float32)


def last_kernel(nf, done, acc, table, rbuf, out_hbm, staged, sem):
    size = nf // QUARTERS
    quarter = lax.axis_index("freq") // size
    far_mid = 1 + 1 - quarter // 2
    nt = acc.shape[0]
    c = out_hbm.shape[1]
    rows = done.shape[0]

    first = pltpu.make_async_copy(done, out_hbm.at[pl.ds(0, rows)], sem.at[0])
    first.start()
    copies = [first]
    part = acc.shape[1] // HALVES
    for h in range(1, HALVES):
        right = half_block(rbuf, far_mid, h, size)
        for s in range(part // c):
            low = h * part + s * c
            block = acc[:, low:low + c] + jnp.dot(
                table[...], right[:, s * c:(s + 1) * c], preferred_element_type=jnp.float32
            )
            place = low // c * nt
            staged[place - rows:place - rows + nt, :] = block.astype(staged.dtype)
            copy = pltpu.make_async_copy(
                staged.at[pl.ds(place - rows, nt)], out_hbm.at[pl.ds(place, nt)], sem.at[len(copies)]
            )
            copy.start()
            copies.append(copy)
    for copy in copies:
        copy.wait()


def kernel(
    nf, ng, kc,
    owners_hbm, tr_hbm, ad_hbm, lo_hbm, pv_hbm, inv_hbm, done, acc, last_table, rbuf,
    owners, tr, ad, lo, pv, inv, spec, sbuf, table,
    joined, known, ready, part_sem, in_sem, owners_sem, lo_sem, pv_sem, inv_sem, own_sem,
    send_sem, recv_sem, psend_sem, precv_sem,
):
    f32, bf16 = jnp.float32, jnp.bfloat16
    kl, _, sl, _ = tr.shape
    c = ad.shape[3]
    nch = kl // kc
    s_loc = sl // nf
    nt, width = acc.shape
    size = nf // QUARTERS
    me = lax.axis_index("freq")
    grp = lax.axis_index("grp")
    quarter = me // size
    place = lax.rem(me, size)
    end = 1 - lax.rem(quarter // 2 + lax.rem(quarter, 2), 2)
    near = flip(quarter, 1)
    across = flip(quarter, 2)
    other = flip(across, 1)
    far_end = across + end * (other - across)
    far_mid = other + end * (across - other)
    early = 2 * (1 - quarter // 2)
    late = early + 1
    odd = lax.rem(quarter, 2)

    def device(q, i):
        return q * size + lax.rem(place + i, size)

    part = max(1, kc // PARTS)

    def first_loads(p):
        rows = pl.ds(p * part, part)
        return (
            pltpu.make_async_copy(tr_hbm.at[rows], tr.at[rows], part_sem.at[p, 0]),
            pltpu.make_async_copy(ad_hbm.at[rows], ad.at[rows], part_sem.at[p, 1]),
        )

    def loads(j):
        rows = pl.ds(j * kc, kc)
        return (
            pltpu.make_async_copy(tr_hbm.at[rows], tr.at[rows], in_sem.at[j, 0]),
            pltpu.make_async_copy(ad_hbm.at[rows], ad.at[rows], in_sem.at[j, 1]),
        )

    lo_copy = pltpu.make_async_copy(lo_hbm, lo, lo_sem)
    owners_copy = pltpu.make_async_copy(owners_hbm, owners, owners_sem)
    pv_copy = pltpu.make_async_copy(pv_hbm, pv.at[grp], pv_sem)
    inv_copy = pltpu.make_async_copy(inv_hbm, inv, inv_sem)

    for p in range(kc // part):
        for copy in first_loads(p):
            copy.start()
    inv_copy.start()

    barrier = pltpu.get_barrier_semaphore()

    def greet(sem, q, skip=0):
        for i in range(skip, size):
            pl.semaphore_signal(sem, inc=1, device_id={"freq": device(q, i)}, device_id_type=MESH)

    def greet_groups(sem):
        for step in range(1, ng):
            pl.semaphore_signal(
                sem, inc=1, device_id={"grp": lax.rem(grp + step, ng)}, device_id_type=MESH
            )

    greet(barrier, across)
    greet(barrier, other)
    greet(barrier, quarter, 1)

    @pl.when(end == 0)
    def _():
        greet(barrier, near)

    @pl.when(end == 1)
    def _():
        greet_groups(barrier)

    def spectra(j, parts=False):
        for i in range(kc):
            if parts and i % part == 0:
                for copy in first_loads(i // part):
                    copy.wait()
            k = j * kc + i
            right = jnp.concatenate([ad[k, 0], ad[k, 1]], axis=1)
            left = jnp.concatenate([tr[k, 0], tr[k, 1]], axis=0)
            both = jnp.dot(left, right, preferred_element_type=f32)
            spec[0, pl.ds(i * sl, sl), :] = both[:sl, :c] - both[sl:, c:]
            spec[1, pl.ds(i * sl, sl), :] = both[:sl, c:] + both[sl:, :c]
        if parts:
            inv_copy.wait()

    def pack(j, d):
        rows = pl.ds(pl.multiple_of(j * 2 * kc, 2 * kc), 2 * kc)
        blocks = []
        for s in range(s_loc):
            picked = pl.ds(d * s_loc + s, kc, stride=sl)
            blocks += [spec[0, picked, :], spec[1, picked, :]]
        block = jnp.concatenate(blocks, axis=0).astype(bf16)
        scaled = jnp.dot(block, inv[...], preferred_element_type=f32).astype(bf16)
        for s in range(s_loc):
            h, column = s // (s_loc // HALVES), s % (s_loc // HALVES) * c
            sbuf[d, h, rows, column:column + c] = scaled[s * 2 * kc:(s + 1) * 2 * kc, :]

    def pack_first(j):
        for i in range(size):
            pack(j, device(early, i))

    def pack_rest(j):
        for q in (late, near, quarter):
            for i in range(size):
                pack(j, device(q, i))

    def send(q, i, which, index):
        dest = device(q, i)
        return pltpu.make_async_remote_copy(
            src_ref=sbuf.at[(dest, *index)],
            dst_ref=rbuf.at[(me, *index)],
            send_sem=send_sem.at[dest, which],
            recv_sem=recv_sem.at[me, which],
            device_id={"freq": dest},
            device_id_type=MESH,
        )

    def arrival(src, which, index):
        return pltpu.make_async_remote_copy(
            src_ref=sbuf.at[(src, *index)],
            dst_ref=rbuf.at[(src, *index)],
            send_sem=send_sem.at[src, which],
            recv_sem=recv_sem.at[src, which],
            device_id={"freq": src},
            device_id_type=MESH,
        )

    everything = slice(None)

    def chunk_rows(j, n=1):
        return (everything, pl.ds(pl.multiple_of(j * 2 * kc, 2 * kc), n * 2 * kc))

    lead = min(LEAD, nch - 1)
    head = (everything, pl.ds(0, lead * 2 * kc))

    def tail(h, n):
        return (h, pl.ds(n * 2 * kc, (nch - n) * 2 * kc))

    def send_group(q, j, which, n=1):
        for i in range(size):
            send(q, i, which, chunk_rows(j, n)).start()

    def send_tails(n):
        for h in range(HALVES):
            for i in range(size):
                send(late, i, h, tail(h, n)).start()

    def late_index(n):
        return [(h, tail(h, n)) for h in range(HALVES)] + ([(HALVES, head)] if n else [])

    own_copy = pltpu.make_async_copy(sbuf.at[me], rbuf.at[me], own_sem)

    def pivot_copy(step, slot):
        return pltpu.make_async_remote_copy(
            src_ref=pv_hbm,
            dst_ref=pv.at[slot],
            send_sem=psend_sem.at[step],
            recv_sem=precv_sem.at[step],
            device_id={"grp": lax.rem(grp + step, ng)},
            device_id_type=MESH,
        )

    for j in range(1, min(AHEAD, nch)):
        for copy in loads(j):
            copy.start()
    group = max(1, nch // NEAR_MESSAGES)

    def sends(j):
        send_group(early, j, 0)
        if lead:
            @pl.when(end == 0)
            def _():
                @pl.when(j < lead)
                def _():
                    send_group(late, j, HALVES)

        @pl.when(lax.rem(j, group) == group - 1)
        def _():
            @pl.when(jnp.logical_and(end == 0, j == group - 1))
            def _():
                pl.semaphore_wait(ready, size)
            send_group(near, j - (group - 1), 0, group)

    spectra(0, parts=True)
    pack_first(0)
    pack_rest(0)
    pl.semaphore_wait(barrier, nf - 1 + end * (ng - 1) - (1 - end) * size)

    @pl.when(end == 1)
    def _():
        greet(ready, near)
        greet_groups(joined)

    @pl.loop(0, nch)
    def _(j):
        @pl.when(j > 0)
        def _():
            @pl.when(j + AHEAD - 1 < nch)
            def _():
                for copy in loads(j + AHEAD - 1):
                    copy.start()

            for copy in loads(j):
                copy.wait()
            spectra(j)
            pack_first(j)
            pack_rest(j)
        sends(j)

    @pl.when(end == 1)
    def _():
        send_tails(0)

    @pl.when(end == 0)
    def _():
        send_tails(lead)

    @pl.when(end == 1)
    def _():
        pl.semaphore_wait(joined, ng - 1)
        greet(known, near)

    @pl.when(end == 0)
    def _():
        pl.semaphore_wait(known, size)

    for i in range(1, size):
        send(quarter, i, 0, (everything,)).start()
    own_copy.start()

    owners_copy.start()
    pv_copy.start()
    lo_copy.start()
    for step in range(1, ng):
        pivot_copy(step, grp).start()

    cols = size * 2 * kl
    coarse = nt // COARSE
    scale = 1.0 / math.sqrt(kl * nf)
    turn = 2.0 * math.pi / nt

    def make_table(q, ref):
        def phase(rows, step, shift):
            col = lax.broadcasted_iota(jnp.int32, (rows, cols), 1)
            row = lax.broadcasted_iota(jnp.int32, (rows, cols), 0) * step
            kk = q * size * kl + (col // (2 * kc)) * kc + col % kc
            imaginary = (col // kc) % 2
            turns = kk * row + imaginary * shift
            return (turns % nt).astype(f32) * turn

        high = phase(coarse, COARSE, 0)
        low = phase(COARSE, 1, nt // 4)
        cos_high, sin_high = jnp.cos(high) * scale, jnp.sin(high) * scale
        cos_low, sin_low = jnp.cos(low), jnp.sin(low)
        for a in range(coarse):
            value = cos_high[a:a + 1] * cos_low - sin_high[a:a + 1] * sin_low
            ref[a * COARSE:(a + 1) * COARSE, :] = value.astype(bf16)

    @pl.loop(0, QUARTERS)
    def _(q):
        make_table(q, table.at[q])
    make_table(far_mid, last_table)

    lo_copy.wait()
    owners_copy.wait()
    pv_copy.wait()
    for step in range(1, ng):
        pivot_copy(step, lax.rem(grp + ng - step, ng)).wait_recv()
    panels = lo.shape[1] // c
    pivots = jnp.concatenate(
        [pv[owners[p], :, p * c:(p + 1) * c] for p in range(panels)], axis=1
    )
    turned = jnp.transpose(inv[...].astype(f32)).astype(bf16)
    scaled_pivots = jnp.dot(turned, pivots, preferred_element_type=f32).astype(bf16)
    tile = min(TILE, nt)

    for s in range(s_loc):
        @pl.loop(0, nt // tile)
        def _(i):
            rows = lo[pl.ds(pl.multiple_of(s * nt + i * tile, tile), tile), :]
            update = lax.dot_general(
                rows, scaled_pivots, (((1,), (1,)), ((), ())), preferred_element_type=f32
            )
            acc[pl.ds(pl.multiple_of(i * tile, tile), tile), s * c:(s + 1) * c] = -update

    def term(q, i):
        rows = pl.ds(pl.multiple_of(i * tile, tile), tile)
        right = jnp.concatenate([half_block(rbuf, q, h, size) for h in range(HALVES)], axis=1)
        return acc[rows, :] + jnp.dot(table[q, rows, :], right, preferred_element_type=f32)

    def add(q):
        @pl.loop(0, nt // tile)
        def _(i):
            acc[pl.ds(pl.multiple_of(i * tile, tile), tile), :] = term(q, i)

    def wait_all(q):
        for i in range(size):
            arrival(q * size + i, 0, (everything,)).wait_recv()

    def wait_half(q, h, n):
        for i in range(size):
            if n and h == 0:
                arrival(q * size + i, HALVES, head).wait_recv()
            arrival(q * size + i, h, tail(h, n)).wait_recv()

    own_copy.wait()
    for i in range(1, size):
        arrival(device(quarter, i), 0, (everything,)).wait_recv()
    add(quarter)

    wait_all(near)
    add(near)

    @pl.when(odd == 0)
    def _():
        wait_all(far_end)

    @pl.when(odd == 1)
    def _():
        for h in range(HALVES):
            wait_half(far_end, h, 0)
    add(far_end)

    for i in range(size):
        for q in (early, near):
            send(q, i, 0, (everything,)).wait_send()
    for i in range(1, size):
        send(quarter, i, 0, (everything,)).wait_send()

    @pl.when(odd == 0)
    def _():
        wait_all(far_mid)

    @pl.when(odd == 1)
    def _():
        wait_half(far_mid, 0, lead)

    part_width = width // HALVES
    value = finished(acc, last_table, rbuf, far_mid, 0, size).astype(bf16)
    for s in range(part_width // c):
        done[s * nt:(s + 1) * nt, :] = value[:, s * c:(s + 1) * c]

    @pl.when(odd == 1)
    def _():
        for h in range(1, HALVES):
            wait_half(far_mid, h, lead)

    @pl.when(end == 1)
    def _():
        for i in range(size):
            for which, index in late_index(0):
                send(late, i, which, index).wait_send()

    @pl.when(end == 0)
    def _():
        for i in range(size):
            for which, index in late_index(lead):
                send(late, i, which, index).wait_send()
    for step in range(1, ng):
        pivot_copy(step, grp).wait_send()


def per_device(nf, ng, transfer, adjoint, lower_rows, pivot_store, owners, inverse_factor):
    kl, _, sl, m = transfer.shape
    c = adjoint.shape[3]
    kc = min(CHUNK, kl)
    nch = kl // kc
    s_loc = sl // nf
    size = nf // QUARTERS
    rows = lower_rows.shape[0]
    nt = rows // s_loc
    bf16 = jnp.bfloat16
    in_hbm = lambda x: pltpu.with_memory_space_constraint(x, pltpu.HBM)
    dma = pltpu.SemaphoreType.DMA
    width = s_loc * c
    cols = size * 2 * kl
    vmem = pl.BlockSpec(memory_space=pltpu.VMEM)
    outs = [
        jax.ShapeDtypeStruct((rows // HALVES, c), bf16),
        jax.ShapeDtypeStruct((nt, width), jnp.float32),
        jax.ShapeDtypeStruct((nt, cols), bf16),
        jax.ShapeDtypeStruct((nf, HALVES, 2 * kl, width // HALVES), bf16),
    ]
    held = sum(math.prod(out.shape) * out.dtype.itemsize for out in outs)
    parts = pl.pallas_call(
        functools.partial(kernel, nf, ng, kc),
        out_shape=outs,
        in_specs=[pl.BlockSpec(memory_space=pltpu.HBM)] * 6,
        out_specs=[vmem] * len(outs),
        scratch_shapes=[
            pltpu.SMEM(owners.shape, jnp.int32),
            pltpu.VMEM(transfer.shape, bf16),
            pltpu.VMEM(adjoint.shape, bf16),
            pltpu.VMEM(lower_rows.shape, bf16),
            pltpu.VMEM((ng,) + pivot_store.shape, bf16),
            pltpu.VMEM(inverse_factor.shape, bf16),
            pltpu.VMEM((2, kc * sl, c), jnp.float32),
            pltpu.VMEM((nf, HALVES, 2 * kl, width // HALVES), bf16),
            pltpu.VMEM((QUARTERS, nt, cols), bf16),
            pltpu.SemaphoreType.REGULAR,
            pltpu.SemaphoreType.REGULAR,
            pltpu.SemaphoreType.REGULAR,
            dma((PARTS, 2)), dma((nch, 2)), dma, dma, dma, dma, dma,
            dma((nf, HALVES + 1)), dma((nf, HALVES + 1)), dma((ng,)), dma((ng,)),
        ],
        compiler_params=pltpu.CompilerParams(
            collective_id=0, has_side_effects=True, vmem_limit_bytes=VMEM_BYTES - held - SPARE
        ),
    )(in_hbm(owners), transfer, adjoint, lower_rows, in_hbm(pivot_store), in_hbm(inverse_factor))
    return pl.pallas_call(
        functools.partial(last_kernel, nf),
        out_shape=jax.ShapeDtypeStruct((rows, c), bf16),
        in_specs=[vmem] * len(outs),
        out_specs=pl.BlockSpec(memory_space=pltpu.HBM),
        scratch_shapes=[pltpu.VMEM((rows - rows // HALVES, c), bf16), dma((1 + s_loc,))],
        compiler_params=pltpu.CompilerParams(vmem_limit_bytes=LAST_BYTES),
    )(*parts)


def solution(mesh):
    nf, ng = mesh.shape["freq"], mesh.shape["grp"]
    in_specs = (
        P("freq", None, "grp", None),
        P("freq", None, None, None),
        P(("grp", "freq"), None),
        P("grp", None),
        P(),
        P(),
    )
    out_specs = P(("grp", "freq"), None)
    return jax.shard_map(
        functools.partial(per_device, nf, ng),
        mesh=mesh, in_specs=in_specs, out_specs=out_specs, check_vma=False,
    )
```

time: 31.1 us -> 29.3 us (0.942)
  local copies, waits for them, and re-layouts: 0.97 us -> 0 us
  Pallas kernels: 29.9 us -> 29.2 us
    unnamed x1 -> x0, local copies, waits for them, and re-layouts: 0.97 us -> none
    pallas_call x1 -> x2, Pallas kernels: 29.9 us -> 29.2 us  [the longest x1 27.9 us: per_device(): pl.pallas_call(functools.partial(kernel, nf, ng, kc), out_shape=outs, in_...]
where the time goes in v2:
time: 29.3 us; the launch traced here: 29.2 us
  Pallas kernels  29.2 us (100%)
    pallas_call x1, Pallas kernels, per_device(): pl.pallas_call(functools.partial(kernel, nf, ng, kc), out_shape=outs, in_...  27.9 us
    pallas_call x1, Pallas kernels, per_device(): pl.pallas_call(functools.partial(last_kernel, nf), out_shape=jax.ShapeDty...  1.29 us

profile of v2, /device:TPU:9, one launch (start us, length us, event | category | flops | bytes accessed | tf_op | source)
XLA Modules:
  0.0 29.2 jit_solution(14412981160539411838)
XLA Ops:
  0.0 27.9 %shard_map.64 = (bf16[2048,128]{1,0:T(8,128)(2,1)S(1)}, f32[1024,512]{1,0:T(8,128)S(1)}, bf16[1024,256]{1,0:T(8,128)(2,1)S(1)}, bf16[8,2,128,256]{3,2,1,0:T(8,128)(2,1)S(1)}) custom-call(s32[3]{0:T(128)} %owners_hbm.1, bf16[64,2,32,512]{3,2,1,0:T(8,128)(2,1)} %tr_hbm.1, bf16[64,2,512,128]{3,2,1,0:T(8,128)(2,1)} %ad_hbm.1, bf16[4096,384]{1,0:T(8,128)(2,1)} %lo_hbm.1, ...), custom_call_target="tpu_custom_call" | custom-call | tf_op jit(solution)/shard_map/pallas_call | solution.py:465
  27.9 1.3 %shard_map.65 = bf16[4096,128]{1,0:T(8,128)(2,1)} custom-call(bf16[2048,128]{1,0:T(8,128)(2,1)S(1)} %get-tuple-element.9.done, f32[1024,512]{1,0:T(8,128)S(1)} %get-tuple-element.10.acc, bf16[1024,256]{1,0:T(8,128)(2,1)S(1)} %get-tuple-element.11.table, bf16[8,2,128,256]{3,2,1,0:T(8,128)(2,1)S(1)} %get-tuple-element.12.rbuf), custom_call_target="tpu_custom_call" | custom-call | tf_op jit(solution)/shard_map/pallas_call | solution.py:490
